TPU v7x, 32 devices: a whole 2x2x4 slice. The times are simulated.
32 devices in a mesh: dp: 8 (over y, x, core), mp: 4 (over z).
Axes of the slice: x: 2, y: 2, z: 4, core: 2. Of those that a mesh axis runs over, the one named last changes fastest.
Arguments:
- tokens: bfloat16 [320, 4096], P('dp'), may hold values from -6 to 6
- attn_gain: float32 [4096], replicated, may hold values from 0.1 to 1.9
- head_gain: float32 [4096], replicated, may hold values from 0.1 to 1.9
- qkv_weight: bfloat16 [4096, 3, 4096], P('dp', None, 'mp'), may hold values from -0.09375 to 0.09375
- out_weight: bfloat16 [4096, 4096], P('mp', 'dp'), may hold values from -0.09375 to 0.09375
- head_weight: bfloat16 [4096, 1024], P('mp'), may hold values from -0.09375 to 0.09375
- key_cache: bfloat16 [320, 64, 4096], P('dp', None, 'mp'), may hold values from -400 to 400
- value_cache: bfloat16 [320, 64, 4096], P('dp', None, 'mp'), may hold values from -6 to 6
- parents: int32 [320], P('dp'), may hold values from 0 to 19
- allowed: int32 [320, 2], P('dp'), may hold values from 0 to 7, all different within a row
Outputs:
- new_stream: bfloat16 [320, 4096], P('dp')
- next_logits: float32 [320, 256], P('dp', 'mp')
Inputs may be any that keep to these rules, and one draw needn't show every extreme that they name: `parents`: a beam's parent is a beam of the same query. `allowed`: the 2 block ids of a beam differ.
All inputs are finite; a program needn't handle non-finite values.
Results may differ from a plain program's by a relative error of at most 0.017.
Values may be sent and summed in bfloat16 or wider, within the bound.
No kernel may reach another device: no remote copies, remote signals or barrier semaphores. Data moves between devices by JAX's collectives and lax.ppermute only.
A program may use at most 128 MiB of HBM per device.

v0:
```python
import jax
import jax.numpy as jnp
from jax import lax
from jax.sharding import PartitionSpec as P

HEAD = 128
BEAMS = 20
BLOCK = 128


def root_norm(values, gain_vec):
    float_values = values.astype(jnp.float32)
    factor = lax.rsqrt(jnp.mean(float_values * float_values, axis=-1, keepdims=True) + 1e-06)
    return float_values * factor * gain_vec


def select_blocks(whole_logits, allowed):
    block_count = whole_logits.shape[1] // BLOCK
    block_list = whole_logits.reshape(whole_logits.shape[0], block_count, BLOCK)
    one_hot_rows = (
        allowed[:, :, None] == jnp.arange(block_count, dtype=jnp.int32)[None, None, :]
    ).astype(jnp.float32)
    selected_token = jnp.einsum(
        "ioh,ihp->iop", one_hot_rows, block_list, precision=lax.Precision.HIGHEST
    )
    return selected_token.reshape(whole_logits.shape[0], -1)


def on_device(
    tokens,
    attn_gain,
    head_gain,
    qkv_weight,
    out_weight,
    head_weight,
    key_cache,
    value_cache,
    parents,
    allowed,
):
    row_count = tokens.shape[0]
    normed = root_norm(tokens, attn_gain).astype(jnp.bfloat16)
    spread = lax.all_to_all(normed, "dp", split_axis=1, concat_axis=0, tiled=True)
    depth_part = qkv_weight.shape[0]
    head_width = qkv_weight.shape[2]
    flat_qkv = qkv_weight.reshape(depth_part, 3 * head_width)
    projected = lax.psum_scatter(
        jnp.dot(spread, flat_qkv, preferred_element_type=jnp.float32),
        "dp",
        scatter_dimension=0,
        tiled=True,
    )
    projected = projected.astype(jnp.bfloat16).reshape(row_count, 3, head_width)
    local_heads = head_width // HEAD
    length = key_cache.shape[1] + 1
    source = jnp.arange(row_count, dtype=jnp.int32) // BEAMS * BEAMS + parents
    key_rows = jnp.concatenate(
        [jnp.take(key_cache, source, axis=0), projected[:, 1][:, None]], axis=1
    )
    value_rows = jnp.concatenate(
        [jnp.take(value_cache, source, axis=0), projected[:, 2][:, None]], axis=1
    )
    key_rows = key_rows.reshape(row_count, length, local_heads, HEAD)
    value_rows = value_rows.reshape(row_count, length, local_heads, HEAD)
    queries = projected[:, 0].reshape(row_count, local_heads, HEAD)
    scores = jnp.einsum(
        "thd,tjhd->thj", queries, key_rows, preferred_element_type=jnp.float32
    ) * HEAD ** (-0.5)
    softmax_w = jax.nn.softmax(scores, axis=-1).astype(jnp.bfloat16)
    attention_result = jnp.einsum(
        "thj,tjhd->thd", softmax_w, value_rows, preferred_element_type=jnp.float32
    )
    attention_result = attention_result.astype(jnp.bfloat16).reshape(row_count, head_width)
    partial_value = jnp.dot(
        attention_result,
        lax.all_gather(out_weight, "dp", axis=1, tiled=True),
        preferred_element_type=jnp.float32,
    )
    attn_out = lax.psum(partial_value, "mp")
    stream = tokens.astype(jnp.float32) + attn_out
    head_input = root_norm(stream, head_gain).astype(jnp.bfloat16)
    depth_rows = head_weight.shape[0]
    own_part = lax.dynamic_slice_in_dim(
        head_input, lax.axis_index("mp") * depth_rows, depth_rows, 1
    )
    partial_logits = jnp.dot(own_part, head_weight, preferred_element_type=jnp.float32)
    next_logits = lax.psum_scatter(
        select_blocks(partial_logits, allowed).astype(jnp.bfloat16),
        "mp",
        scatter_dimension=1,
        tiled=True,
    ).astype(jnp.float32)
    return (stream.astype(jnp.bfloat16), next_logits)


def solution(mesh):
    in_specs = (
        P("dp", None),
        P(),
        P(),
        P("dp", None, "mp"),
        P("mp", "dp"),
        P("mp", None),
        P("dp", None, "mp"),
        P("dp", None, "mp"),
        P("dp"),
        P("dp", None),
    )
    out_specs = (P("dp", None), P("dp", "mp"))
    return jax.shard_map(
        on_device, mesh=mesh, in_specs=in_specs, out_specs=out_specs, check_vma=False
    )
```

profile of v0, /device:TPU:0, one launch (start us, length us, event | category | flops | bytes accessed | tf_op | source)
XLA Modules:
  0.0 211.9 jit_solution(16103499963755374255)
XLA Ops:
  7.2 1.3 fusion.11
  8.5 1.1 fusion.13
  9.6 0.7 copy.55
  10.4 5.2 %all-to-all-start = ((bf16[40,8,512]{2,0,1:T(8,128)(2,1)}), bf16[40,8,512]{2,0,1:T(8,128)(2,1)S(1)}, u32[]{:S(2)}, u32[]{:S(2)}) async-start(bf16[40,8,512]{2,0,1:T(8,128)(2,1)} %bitcast.32), calls=%async_computation | async-start | bytes 655360 | tf_op jit(solution)/shard_map/all_to_all | solution.py:43
  15.6 4.7 %copy.24 = bf16[512,3,1024]{0,2,1:T(8,128)(2,1)} copy(bf16[512,3,1024]{2,0,1:T(8,128)(2,1)} %param.15) | data formatting | bytes 6291456 | tf_op args[3]
  20.3 2.9 %all-to-all-done = bf16[40,8,512]{2,0,1:T(8,128)(2,1)S(1)} async-done(((bf16[40,8,512]{2,0,1:T(8,128)(2,1)}), bf16[40,8,512]{2,0,1:T(8,128)(2,1)S(1)}, u32[]{:S(2)}, u32[]{:S(2)}) %all-to-all-start) | async-done | bytes 327712 | tf_op jit(solution)/shard_map/all_to_all | solution.py:43
  23.2 5.0 %fusion.35 = f32[320,3072]{1,0:T(8,128)} fusion(bf16[320,512]{1,0:T(8,128)(2,1)S(1)} %bitcast.34, bf16[512,3072]{0,1:T(8,128)(2,1)} %bitcast.33), kind=kOutput, calls=%fused_computation.57 | convolution fusion | flops 1006632960 | bytes 7405568 | tf_op jit(solution)/shard_map/dot_general | solution.py:48
  28.3 0.7 all-gather.2.cloned.1.call-update
  29.1 7.2 %gather_fusion = bf16[40,64,1024]{2,1,0:T(8,128)(2,1)} fusion(bf16[40,64,1024]{2,1,0:T(8,128)(2,1)} %param.18, s32[1024]{0:T(1024)S(1)} %pad_clamp_fusion), kind=kCustom, calls=%fused_computation.clone | custom fusion | bytes 10485920 | tf_op jit(solution)/shard_map/jit(_take)/gather | solution.py:58
  36.3 7.6 %gather_fusion.1 = bf16[40,64,1024]{2,1,0:T(8,128)(2,1)} fusion(bf16[40,64,1024]{2,1,0:T(8,128)(2,1)} %param.19, s32[1024]{0:T(1024)S(1)} %pad_clamp_fusion), kind=kCustom, calls=%fused_computation.1.clone | custom fusion | bytes 10485920 | tf_op jit(solution)/shard_map/jit(_take)/gather | solution.py:61
  43.9 9.1 %broadcast_select_fusion.1 = (bf16[40,64,1024]{2,1,0:T(8,128)(2,1)}, bf16[40,64,1024]{2,1,0:T(8,128)(2,1)}) fusion(bf16[40,64,1024]{2,1,0:T(8,128)(2,1)} %gather_fusion, pred[40]{0:T(512)(128)(4,1)S(1)} %get-tuple-element.5, bf16[40,64,1024]{2,1,0:T(8,128)(2,1)} %gather_fusion.1), kind=kLoop, calls=%fused_computation.11 | loop fusion | flops 5242880 | bytes 20971560 | tf_op jit(solution)/shard_map/jit(_take)/select_n | solution.py:58
  52.9 24.6 %reduce-scatter.5.cloned.1.call-done = f32[40,3072]{1,0:T(8,128)} async-done(((f32[320,3072]{1,0:T(8,128)}), f32[40,3072]{1,0:T(8,128)}) %reduce-scatter.5.cloned.1.call-update) | async-done | bytes 491536 | tf_op jit(solution)/shard_map/reduce_scatter | solution.py:47
  77.6 1.1 convert_element_type.34
  78.6 0.4 reshape.54
  79.0 0.3 fusion.32
  79.3 11.1 %pad_maximum_fusion = (bf16[40,65,1024]{2,1,0:T(8,128)(2,1)}, bf16[40,65,1024]{2,1,0:T(8,128)(2,1)}) fusion(bf16[40,1,1024]{2,1,0:T(2,128)(2,1)S(1)} %get-tuple-element.7, bf16[40,64,1024]{2,1,0:T(8,128)(2,1)} %get-tuple-element.9, bf16[40,1,1024]{2,1,0:T(2,128)(2,1)S(1)} %get-tuple-element.8, bf16[40,64,1024]{2,1,0:T(8,128)(2,1)} %get-tuple-element.10), kind=kLoop, calls=%fused_computation.4 | loop fusion | flops 21299200 | bytes 21299200 | tf_op jit(solution)/shard_map/concatenate | solution.py:57
  90.4 9.1 %reshape.86 = bf16[40,65,8,128]{3,2,1,0:T(8,128)(2,1)} reshape(bf16[40,65,1024]{2,1,0:T(8,128)(2,1)} %get-tuple-element.11) | data formatting | bytes 10649600 | tf_op jit(solution)/shard_map/reshape | solution.py:63
  99.5 9.3 %reshape.87 = bf16[40,65,8,128]{3,2,1,0:T(8,128)(2,1)} reshape(bf16[40,65,1024]{2,1,0:T(8,128)(2,1)} %get-tuple-element.12) | data formatting | bytes 10649600 | tf_op jit(solution)/shard_map/reshape | solution.py:64
  108.8 5.9 %fusion.4 = f32[40,8,1,65]{3,2,1,0:T(1,128)S(1)} fusion(bf16[40,65,8,128]{3,2,1,0:T(8,128)(2,1)} %reshape.86, bf16[40,3,1024]{2,1,0:T(4,128)(2,1)S(1)} %reshape.54), kind=kOutput, calls=%fused_computation.8 | convolution fusion | flops 5324800 | bytes 5571840 | tf_op jit(solution)/shard_map/thd,tjhd->thj/dot_general | solution.py:66
  114.9 4.2 %fusion.2 = f32[40,8,1,128]{3,2,1,0:T(1,128)S(1)} fusion(bf16[40,65,8,128]{3,2,1,0:T(8,128)(2,1)} %reshape.87, bf16[40,8,65,1]{2,1,0,3:T(8,128)(2,1)S(1)} %fusion.10), kind=kOutput, calls=%fused_computation.6 | convolution fusion | flops 5324800 | bytes 5530240 | tf_op jit(solution)/shard_map/thj,tjhd->thd/dot_general | solution.py:70
  119.1 16.2 %all-gather.2.cloned.1.call-done = bf16[1024,4096]{1,0:T(8,128)(2,1)} async-done(((bf16[1024,512]{1,0:T(8,128)(2,1)}), bf16[1024,4096]{1,0:T(8,128)(2,1)}) %all-gather.2.cloned.1.call-update) | async-done | bytes 8388624 | tf_op jit(solution)/shard_map/all_gather | solution.py:76
  135.3 5.9 %fusion.19 = f32[40,4096]{1,0:T(8,128)} fusion(bf16[1024,4096]{1,0:T(8,128)(2,1)} %all-gather.2.cloned.1.call-done, bf16[5,8,8,128]{3,2,1,0:T(8,128)(2,1)S(1)} %bitcast.36), kind=kOutput, calls=%fused_computation.34 | convolution fusion | flops 335544320 | bytes 9125888 | tf_op jit(solution)/shard_map/dot_general | solution.py:74
  141.4 0.7 dynamic-slice
  142.1 39.9 %all-reduce.2.cloned.1.call-done = f32[40,4096]{1,0:T(8,128)} async-done(((f32[40,4096]{1,0:T(8,128)}), f32[40,4096]{1,0:T(8,128)}) %all-reduce.2.cloned.1.call-update) | async-done | bytes 655376 | tf_op jit(solution)/shard_map/psum | solution.py:79
  181.9 1.3 multiply_reduce_fusion
  183.2 0.5 convolution_bitcast_fusion
  183.8 0.3 convolution_convert_fusion
  184.1 0.7 copy.40
  184.9 0.8 convert_element_type.37
  185.7 18.2 %reduce-scatter.7.cloned.1.call-done = bf16[64,40]{1,0:T(8,128)(2,1)} async-done(((bf16[256,40]{1,0:T(8,128)(2,1)}), bf16[64,40]{1,0:T(8,128)(2,1)}) %reduce-scatter.7.cloned.1.call-update) | async-done | bytes 5136
  203.9 0.8 copy.39
  204.7 0.6 convert_element_type.41
  (23 shorter events, 0.6 us)
Async XLA Ops:
  7.2 176.1 %copy-start = (bf16[1024,1024]{1,0:T(8,128)(2,1)S(1)}, bf16[1024,1024]{1,0:T(8,128)(2,1)}, u32[]{:S(2)}) copy-start(bf16[1024,1024]{1,0:T(8,128)(2,1)} %param.17) | copy-start | bytes 6291460
  10.4 12.8 %all-to-all-start = ((bf16[40,8,512]{2,0,1:T(8,128)(2,1)}), bf16[40,8,512]{2,0,1:T(8,128)(2,1)S(1)}, u32[]{:S(2)}, u32[]{:S(2)}) async-start(bf16[40,8,512]{2,0,1:T(8,128)(2,1)} %bitcast.32), calls=%async_computation | async-start | bytes 655360 | tf_op jit(solution)/shard_map/all_to_all | solution.py:43
  15.6 62.0 %reduce-scatter.5.cloned.1.call-start = ((), (), s32[]{:S(2)}) async-start(), calls=%async_computation.3 | async-start | bytes 4423680 | tf_op jit(solution)/shard_map/reduce_scatter | solution.py:47
  23.2 5.8 %copy-start.3 = (s32[40]{0:T(128)S(1)}, s32[40]{0:T(128)}, u32[]{:S(2)}) copy-start(s32[40]{0:T(128)} %param.20) | copy-start | bytes 484
  28.2 107.1 %all-gather.2.cloned.1.call-start = ((), (), s32[]{:S(2)}) async-start(), calls=%async_computation.4 | async-start | bytes 9437184 | tf_op jit(solution)/shard_map/all_gather | solution.py:76
  29.0 153.0 %all-reduce.2.cloned.1.call-start = ((), (), s32[]{:S(2)}) async-start(), calls=%async_computation.5 | async-start | bytes 1310720 | tf_op jit(solution)/shard_map/psum | solution.py:79
  135.3 6.0 %copy-start.2 = (s32[40,2]{0,1:T(2,128)S(1)}, s32[40,2]{0,1:T(2,128)}, u32[]{:S(2)}) copy-start(s32[40,2]{0,1:T(2,128)} %param.21) | copy-start | bytes 964
  135.3 46.6 %copy-start.1 = (bf16[40,4096]{1,0:T(8,128)(2,1)S(1)}, bf16[40,4096]{1,0:T(8,128)(2,1)}, u32[]{:S(2)}) copy-start(bf16[40,4096]{1,0:T(8,128)(2,1)} %param.12) | copy-start | bytes 983044
  141.2 62.7 %reduce-scatter.7.cloned.1.call-start = ((), (), s32[]{:S(2)}) async-start(), calls=%async_computation.6 | async-start | bytes 81920
Sparse Core Ops, SparseCore 0:
  28.3 49.1 reduce-scatter.4
  79.4 55.8 all-gather.1
  141.4 40.5 all-reduce.1
  185.0 18.8 reduce-scatter.6
where the time goes:
time: 213 us; the launch traced here: 212 us
  waiting for transfers between devices  103 us (48%)
  local copies, waits for them, and re-layouts  41.6 us (20%)
  other arithmetic  26.6 us (12%)
  matrix products  21.8 us (10%)
  between operations  13.9 us (7%)
  starting transfers between devices  5.36 us (3%)
    psum x1, waiting for transfers between devices, on_device(): attn_out = lax.psum(partial_value, 'mp')  39.9 us
    reduce_scatter x1, waiting for transfers between devices, on_device(): lax.psum_scatter(jnp.dot(spread, flat_qkv, preferred_element_type=jnp.flo...  24.6 us
    unnamed x5, waiting for transfers between devices  19 us
    all_gather x1, waiting for transfers between devices, on_device(): lax.all_gather(out_weight, 'dp', axis=1, tiled=True)  16.2 us
    concatenate x1, other arithmetic, on_device(): jnp.concatenate([jnp.take(key_cache, source, axis=0), projected[:, 1][:,...  11.1 us
    reshape x1, local copies, waits for them, and re-layouts, on_device(): value_rows = value_rows.reshape(row_count, length, local_heads, HEAD)  9.25 us
    reshape x1, local copies, waits for them, and re-layouts, on_device(): key_rows = key_rows.reshape(row_count, length, local_heads, HEAD)  9.11 us
    select_n x1, other arithmetic, on_device(): jnp.take(key_cache, source, axis=0)  9.08 us
  transfers between devices with their start and end apart: 5, of which 5 were waited for; matrix products, arithmetic and copies ran while one was open for 34% of the time, Pallas kernels for 0%

commit v1 on v0

--- a/solution.py
+++ b/solution.py
@@ -6,6 +6,13 @@
 HEAD = 128
 BEAMS = 20
 BLOCK = 128
+
+
+def swapped_in(shard, axis, d):
+    size = lax.axis_size(axis)
+    blocks = jnp.stack([shard for _ in range(size)])
+    blocks = lax.all_to_all(blocks, axis, split_axis=0, concat_axis=0)
+    return jnp.concatenate(blocks, axis=d)
 
 
 def root_norm(values, gain_vec):
@@ -72,9 +79,7 @@
     )
     attention_result = attention_result.astype(jnp.bfloat16).reshape(row_count, head_width)
     partial_value = jnp.dot(
-        attention_result,
-        lax.all_gather(out_weight, "dp", axis=1, tiled=True),
-        preferred_element_type=jnp.float32,
+        attention_result, swapped_in(out_weight, "dp", 1), preferred_element_type=jnp.float32
     )
     attn_out = lax.psum(partial_value, "mp")
     stream = tokens.astype(jnp.float32) + attn_out

time: 213 us -> 249 us (1.17)
  waiting for transfers between devices: 103 us -> 127 us
  starting transfers between devices: 5.36 us -> 10.7 us
  local copies, waits for them, and re-layouts: 41.6 us -> 46.9 us
    reduce_scatter x1, waiting for transfers between devices: 24.6 us -> 47.6 us  [on_device(): lax.psum_scatter(jnp.dot(spread, flat_qkv, preferred_element_type=jnp.flo...]
    psum x1, waiting for transfers between devices: 39.9 us -> 58.4 us  [on_device(): attn_out = lax.psum(partial_value, 'mp')]
    all_gather x1 -> x0, waiting for transfers between devices: 16.2 us -> none  [on_device(): lax.all_gather(out_weight, 'dp', axis=1, tiled=True)]
    all_to_all x0 -> x1, starting transfers between devices: none -> 5.18 us  [swapped_in(): blocks = lax.all_to_all(blocks, axis, split_axis=0, concat_axis=0)]
    another operation x0 -> x1, local copies, waits for them, and re-layouts: none -> 4.3 us  [swapped_in(): blocks = jnp.stack([shard for _ in range(size)])]
    unnamed x13 -> x14, local copies, waits for them, and re-layouts: 6.34 us -> 7.84 us
    unnamed x5 -> x4, waiting for transfers between devices: 19 us -> 18.3 us
  transfers between devices with their start and end apart: 5 -> 5, of which waited for: 5 -> 4; matrix products, arithmetic and copies ran while one was open for 34% -> 31% of each run, Pallas kernels for 0% -> 0%
where the time goes in v1:
time: 249 us; the launch traced here: 248 us
  waiting for transfers between devices  127 us (51%)
  local copies, waits for them, and re-layouts  46.9 us (19%)
  other arithmetic  26.3 us (11%)
  matrix products  22.6 us (9%)
  between operations  13.9 us (6%)
  starting transfers between devices  10.7 us (4%)
    psum x1, waiting for transfers between devices, on_device(): attn_out = lax.psum(partial_value, 'mp')  58.4 us
    reduce_scatter x1, waiting for transfers between devices, on_device(): lax.psum_scatter(jnp.dot(spread, flat_qkv, preferred_element_type=jnp.flo...  47.6 us
    unnamed x4, waiting for transfers between devices  18.3 us
    concatenate x1, other arithmetic, on_device(): jnp.concatenate([jnp.take(key_cache, source, axis=0), projected[:, 1][:,...  11 us
    reshape x1, local copies, waits for them, and re-layouts, on_device(): key_rows = key_rows.reshape(row_count, length, local_heads, HEAD)  9.11 us
    reshape x1, local copies, waits for them, and re-layouts, on_device(): value_rows = value_rows.reshape(row_count, length, local_heads, HEAD)  9.09 us
    select_n x1, other arithmetic, on_device(): jnp.take(key_cache, source, axis=0)  8.92 us
    unnamed x14, local copies, waits for them, and re-layouts  7.84 us
  transfers between devices with their start and end apart: 5, of which 4 were waited for; matrix products, arithmetic and copies ran while one was open for 31% of the time, Pallas kernels for 0%

profile of v1, /device:TPU:0, one launch (start us, length us, event | category | flops | bytes accessed | tf_op | source)
XLA Modules:
  0.0 247.7 jit_solution(12631220784893852910)
XLA Ops:
  7.2 1.3 fusion.11
  8.5 1.1 fusion.13
  9.6 0.7 copy.58
  10.4 5.2 %all-to-all-start = ((bf16[40,8,512]{2,0,1:T(8,128)(2,1)}), bf16[40,8,512]{2,0,1:T(8,128)(2,1)S(1)}, u32[]{:S(2)}, u32[]{:S(2)}) async-start(bf16[40,8,512]{2,0,1:T(8,128)(2,1)} %bitcast.35), calls=%async_computation | async-start | bytes 655360 | tf_op jit(solution)/shard_map/all_to_all | solution.py:50
  15.6 4.7 %copy.26 = bf16[512,3,1024]{0,2,1:T(8,128)(2,1)} copy(bf16[512,3,1024]{2,0,1:T(8,128)(2,1)} %param.15) | data formatting | bytes 6291456 | tf_op args[3]
  20.3 2.9 %all-to-all-done = bf16[40,8,512]{2,0,1:T(8,128)(2,1)S(1)} async-done(((bf16[40,8,512]{2,0,1:T(8,128)(2,1)}), bf16[40,8,512]{2,0,1:T(8,128)(2,1)S(1)}, u32[]{:S(2)}, u32[]{:S(2)}) %all-to-all-start) | async-done | bytes 327712 | tf_op jit(solution)/shard_map/all_to_all | solution.py:50
  23.2 5.0 %fusion.35 = f32[320,3072]{1,0:T(8,128)} fusion(bf16[320,512]{1,0:T(8,128)(2,1)S(1)} %bitcast.37, bf16[512,3072]{0,1:T(8,128)(2,1)} %bitcast.36), kind=kOutput, calls=%fused_computation.57 | convolution fusion | flops 1006632960 | bytes 7405568 | tf_op jit(solution)/shard_map/dot_general | solution.py:55
  28.2 1.5 copy.29
  29.7 4.3 %stack.2 = bf16[8,1024,512]{1,2,0:T(8,128)(2,1)} broadcast(bf16[1024,512]{0,1:T(8,128)(2,1)S(1)} %copy.29), dimensions={1,2} | broadcast | bytes 9437184 | tf_op jit(solution)/shard_map/stack | solution.py:13
  34.0 5.2 %all-to-all-start.1 = ((bf16[8,1024,512]{1,2,0:T(8,128)(2,1)}), bf16[8,1024,512]{1,2,0:T(8,128)(2,1)}, u32[]{:S(2)}, u32[]{:S(2)}) async-start(bf16[8,1024,512]{1,2,0:T(8,128)(2,1)} %stack.2), calls=%async_computation.2 | async-start | bytes 16777216 | tf_op jit(solution)/shard_map/all_to_all | solution.py:14
  39.4 7.4 %gather_fusion = bf16[40,64,1024]{2,1,0:T(8,128)(2,1)} fusion(bf16[40,64,1024]{2,1,0:T(8,128)(2,1)} %param.18, s32[1024]{0:T(1024)S(1)} %pad_clamp_fusion), kind=kCustom, calls=%fused_computation.clone | custom fusion | bytes 10485920 | tf_op jit(solution)/shard_map/jit(_take)/gather | solution.py:65
  46.9 7.1 %gather_fusion.1 = bf16[40,64,1024]{2,1,0:T(8,128)(2,1)} fusion(bf16[40,64,1024]{2,1,0:T(8,128)(2,1)} %param.19, s32[1024]{0:T(1024)S(1)} %pad_clamp_fusion), kind=kCustom, calls=%fused_computation.1.clone | custom fusion | bytes 10485920 | tf_op jit(solution)/shard_map/jit(_take)/gather | solution.py:68
  54.0 8.9 %broadcast_select_fusion.1 = (bf16[40,64,1024]{2,1,0:T(8,128)(2,1)}, bf16[40,64,1024]{2,1,0:T(8,128)(2,1)}) fusion(bf16[40,64,1024]{2,1,0:T(8,128)(2,1)} %gather_fusion, pred[40]{0:T(512)(128)(4,1)S(1)} %get-tuple-element.5, bf16[40,64,1024]{2,1,0:T(8,128)(2,1)} %gather_fusion.1), kind=kLoop, calls=%fused_computation.11 | loop fusion | flops 5242880 | bytes 20971560 | tf_op jit(solution)/shard_map/jit(_take)/select_n | solution.py:65
  62.9 47.6 %reduce-scatter.5.cloned.1.call-done = f32[40,3072]{1,0:T(8,128)} async-done(((f32[320,3072]{1,0:T(8,128)}), f32[40,3072]{1,0:T(8,128)}) %reduce-scatter.5.cloned.1.call-update) | async-done | bytes 491536 | tf_op jit(solution)/shard_map/reduce_scatter | solution.py:54
  110.5 1.1 convert_element_type.34
  111.5 0.4 reshape.62
  112.2 11.0 %pad_maximum_fusion = (bf16[40,65,1024]{2,1,0:T(8,128)(2,1)}, bf16[40,65,1024]{2,1,0:T(8,128)(2,1)}) fusion(bf16[40,1,1024]{2,1,0:T(2,128)(2,1)S(1)} %get-tuple-element.7, bf16[40,64,1024]{2,1,0:T(8,128)(2,1)} %get-tuple-element.9, bf16[40,1,1024]{2,1,0:T(2,128)(2,1)S(1)} %get-tuple-element.8, bf16[40,64,1024]{2,1,0:T(8,128)(2,1)} %get-tuple-element.10), kind=kLoop, calls=%fused_computation.4 | loop fusion | flops 21299200 | bytes 21299200 | tf_op jit(solution)/shard_map/concatenate | solution.py:64
  123.2 9.1 %reshape.96 = bf16[40,65,8,128]{3,2,1,0:T(8,128)(2,1)} reshape(bf16[40,65,1024]{2,1,0:T(8,128)(2,1)} %get-tuple-element.11) | data formatting | bytes 10649600 | tf_op jit(solution)/shard_map/reshape | solution.py:70
  132.3 9.1 %reshape.97 = bf16[40,65,8,128]{3,2,1,0:T(8,128)(2,1)} reshape(bf16[40,65,1024]{2,1,0:T(8,128)(2,1)} %get-tuple-element.12) | data formatting | bytes 10649600 | tf_op jit(solution)/shard_map/reshape | solution.py:71
  141.4 5.6 %fusion.4 = f32[40,8,1,65]{3,2,1,0:T(1,128)S(1)} fusion(bf16[40,65,8,128]{3,2,1,0:T(8,128)(2,1)} %reshape.96, bf16[40,3,1024]{2,1,0:T(4,128)(2,1)S(1)} %reshape.62), kind=kOutput, calls=%fused_computation.8 | convolution fusion | flops 5324800 | bytes 5571840 | tf_op jit(solution)/shard_map/thd,tjhd->thj/dot_general | solution.py:73
  147.3 4.2 %fusion.2 = f32[40,8,1,128]{3,2,1,0:T(1,128)S(1)} fusion(bf16[40,65,8,128]{3,2,1,0:T(8,128)(2,1)} %reshape.97, bf16[40,8,65,1]{2,1,0,3:T(8,128)(2,1)S(1)} %fusion.10), kind=kOutput, calls=%fused_computation.6 | convolution fusion | flops 5324800 | bytes 5530240 | tf_op jit(solution)/shard_map/thj,tjhd->thd/dot_general | solution.py:77
  151.6 6.9 %fusion.19 = f32[40,4096]{1,0:T(8,128)} fusion(bf16[1024,4096]{0,1:T(8,128)(2,1)} %bitcast.10, bf16[5,8,8,128]{3,2,1,0:T(8,128)(2,1)S(1)} %bitcast.39), kind=kOutput, calls=%fused_computation.34 | convolution fusion | flops 335544320 | bytes 9125888 | tf_op jit(solution)/shard_map/dot_general | solution.py:81
  158.7 0.7 dynamic-slice
  159.4 58.4 %all-reduce.2.cloned.1.call-done = f32[40,4096]{1,0:T(8,128)} async-done(((f32[40,4096]{1,0:T(8,128)}), f32[40,4096]{1,0:T(8,128)}) %all-reduce.2.cloned.1.call-update) | async-done | bytes 655376 | tf_op jit(solution)/shard_map/psum | solution.py:84
  217.8 1.3 multiply_reduce_fusion
  219.1 0.5 convolution_bitcast_fusion
  219.7 0.3 convolution_convert_fusion
  220.0 0.7 copy.43
  220.8 0.8 convert_element_type.37
  221.5 18.2 %reduce-scatter.7.cloned.1.call-done = bf16[64,40]{1,0:T(8,128)(2,1)} async-done(((bf16[256,40]{1,0:T(8,128)(2,1)}), bf16[64,40]{1,0:T(8,128)(2,1)}) %reduce-scatter.7.cloned.1.call-update) | async-done | bytes 5136
  239.8 0.8 copy.42
  240.6 0.6 convert_element_type.41
  (24 shorter events, 1.1 us)
Async XLA Ops:
  7.2 212.0 %copy-start = (bf16[1024,1024]{1,0:T(8,128)(2,1)S(1)}, bf16[1024,1024]{1,0:T(8,128)(2,1)}, u32[]{:S(2)}) copy-start(bf16[1024,1024]{1,0:T(8,128)(2,1)} %param.17) | copy-start | bytes 6291460
  10.4 12.8 %all-to-all-start = ((bf16[40,8,512]{2,0,1:T(8,128)(2,1)}), bf16[40,8,512]{2,0,1:T(8,128)(2,1)S(1)}, u32[]{:S(2)}, u32[]{:S(2)}) async-start(bf16[40,8,512]{2,0,1:T(8,128)(2,1)} %bitcast.35), calls=%async_computation | async-start | bytes 655360 | tf_op jit(solution)/shard_map/all_to_all | solution.py:50
  15.6 94.9 %reduce-scatter.5.cloned.1.call-start = ((), (), s32[]{:S(2)}) async-start(), calls=%async_computation.4 | async-start | bytes 4423680 | tf_op jit(solution)/shard_map/reduce_scatter | solution.py:54
  34.0 5.4 %copy-start.3 = (s32[40]{0:T(128)S(1)}, s32[40]{0:T(128)}, u32[]{:S(2)}) copy-start(s32[40]{0:T(128)} %param.20) | copy-start | bytes 484
  34.0 117.6 %all-to-all-start.1 = ((bf16[8,1024,512]{1,2,0:T(8,128)(2,1)}), bf16[8,1024,512]{1,2,0:T(8,128)(2,1)}, u32[]{:S(2)}, u32[]{:S(2)}) async-start(bf16[8,1024,512]{1,2,0:T(8,128)(2,1)} %stack.2), calls=%async_computation.2 | async-start | bytes 16777216 | tf_op jit(solution)/shard_map/all_to_all | solution.py:14
  39.2 178.7 %all-reduce.2.cloned.1.call-start = ((), (), s32[]{:S(2)}) async-start(), calls=%async_computation.5 | async-start | bytes 1310720 | tf_op jit(solution)/shard_map/psum | solution.py:84
  151.5 7.1 %copy-start.2 = (s32[40,2]{0,1:T(2,128)S(1)}, s32[40,2]{0,1:T(2,128)}, u32[]{:S(2)}) copy-start(s32[40,2]{0,1:T(2,128)} %param.21) | copy-start | bytes 964
  151.5 66.3 %copy-start.1 = (bf16[40,4096]{1,0:T(8,128)(2,1)S(1)}, bf16[40,4096]{1,0:T(8,128)(2,1)}, u32[]{:S(2)}) copy-start(bf16[40,4096]{1,0:T(8,128)(2,1)} %param.12) | copy-start | bytes 983044
  158.5 81.2 %reduce-scatter.7.cloned.1.call-start = ((), (), s32[]{:S(2)}) async-start(), calls=%async_computation.6 | async-start | bytes 81920
Sparse Core Ops, SparseCore 0:
  28.3 82.1 reduce-scatter.4
  158.7 59.1 all-reduce.1
  220.9 18.8 reduce-scatter.6
